TPU v7x, 32 devices: a whole 2x2x4 slice. The times are simulated.
32 devices in a mesh: dp: 8 (over y, x, core), group: 4 (over z).
Axes of the slice: x: 2, y: 2, z: 4, core: 2. Of those that a mesh axis runs over, the one named last changes fastest.
Arguments:
- patches: bfloat16 [53248, 768], P('dp', 'group'), may hold values from -4 to 4
- embed_weight: bfloat16 [768, 1024], P('dp', 'group'), may hold values from -0.0625 to 0.0625
- channel_gain: float32 [1024], replicated, may hold values from 0.1 to 1.9
- cotangent: bfloat16 [53248, 1024], P('dp', 'group'), may hold values from -6 to 6
Outputs:
- weight_grad: float32 [768, 1024], P('dp', 'group')
- gain_grad: float32 [1024], P('group')
All inputs are finite; a program needn't handle non-finite values.
Results may differ from a plain program's by a relative error of at most 0.00155.
Values may be sent and summed in bfloat16 or wider, within the bound.
A program may use at most 128 MiB of HBM per device.

v0:
```python
import math

import jax
import jax.numpy as jnp
from jax import lax
from jax.sharding import PartitionSpec as P

GW = 64
ITERS = 5


EPSILON = 1e-05
highest = lax.Precision.HIGHEST


def matmul_batch(left, right):
    return jnp.einsum("gij,gjk->gik", left, right, precision=highest)


def whiten_matrix(covariance):
    width = covariance.shape[-1]
    traces = jnp.trace(covariance, axis1=1, axis2=2)
    normed = covariance / traces[:, None, None]
    iterate = jnp.broadcast_to(jnp.eye(width, dtype=jnp.float32), covariance.shape)
    for counter in range(ITERS):
        cubed = matmul_batch(matmul_batch(iterate, iterate), iterate)
        iterate = 1.5 * iterate - 0.5 * matmul_batch(cubed, normed)
    return iterate / jnp.sqrt(traces)[:, None, None]


def group_products(grouped):
    return jnp.einsum("tga,tgb->gab", grouped, grouped, precision=highest)


def local_backward(grouped, whitener, cot_rows, gain_here, loss_scale):
    tok_rows = grouped.shape[0]
    whitened = jnp.einsum("tgb,gab->tga", grouped, whitener, precision=highest).reshape(
        tok_rows, -1
    )
    grad_scaled = cot_rows.astype(jnp.float32) * loss_scale
    gain_part = jnp.sum(grad_scaled * whitened, axis=0)
    grad_white = (grad_scaled * gain_here).reshape(tok_rows, -1, GW)
    whitener_part = jnp.einsum("tga,tgb->gab", grad_white, grouped, precision=highest)
    return (grad_white, (whitener_part, jnp.sum(grad_white, axis=0), gain_part))


def finish_backward(grouped, grad_white, whitener, pullback, summed, total_tokens):
    tok_rows = grouped.shape[0]
    (grad_cov,) = pullback(summed[0])
    symmetric = (grad_cov + jnp.swapaxes(grad_cov, 1, 2)) / total_tokens
    direct = jnp.einsum("tga,gab->tgb", grad_white, whitener, precision=highest)
    through = jnp.einsum("tgb,gcb->tgc", grouped, symmetric, precision=highest)
    mean_part = jnp.einsum("ga,gab->gb", summed[1], whitener, precision=highest) / total_tokens
    return (direct + through - mean_part).reshape(tok_rows, -1).astype(jnp.bfloat16)


def body(patches, embed_weight, channel_gain, cotangent):
    tok_rows = patches.shape[0]
    total_tokens = tok_rows * lax.axis_size("dp")
    loss_scale = 1.0 / math.sqrt(total_tokens)
    identity = jnp.eye(GW, dtype=jnp.float32)
    width_here = embed_weight.shape[1]
    weights = lax.all_gather(embed_weight, "dp", axis=0, tiled=True)
    full_patches = lax.all_gather(patches, "group", axis=1, tiled=True)
    gain_here = lax.dynamic_slice_in_dim(
        channel_gain, lax.axis_index("group") * width_here, width_here
    )
    embedded = jnp.dot(full_patches, weights, preferred_element_type=jnp.float32).astype(
        jnp.bfloat16
    )
    features = embedded.astype(jnp.float32)
    raw_grouped = features.reshape(tok_rows, -1, GW)
    sum_feat, raw_products = lax.psum(
        (jnp.sum(features, axis=0), group_products(raw_grouped)), "dp"
    )
    average = sum_feat / total_tokens
    mean_groups = average.reshape(-1, GW)
    covariance = (
        raw_products / total_tokens
        - jnp.einsum("ga,gb->gab", mean_groups, mean_groups)
        + EPSILON * identity
    )
    centered = features - average
    grouped = centered.reshape(tok_rows, -1, GW)
    whitener, pullback = jax.vjp(whiten_matrix, covariance)
    grad_white, partials = local_backward(grouped, whitener, cotangent, gain_here, loss_scale)
    summed = lax.psum((partials[0], partials[1], partials[2]), "dp")
    grad_feat = finish_backward(grouped, grad_white, whitener, pullback, summed, total_tokens)
    weight_grad = lax.psum_scatter(
        lax.dot_general(
            full_patches, grad_feat, (((0,), (0,)), ((), ())), preferred_element_type=jnp.float32
        ),
        "dp",
        scatter_dimension=0,
        tiled=True,
    )
    gain_grad = summed[2]
    return (weight_grad, gain_grad)


def solution(mesh):
    placed = (P("dp", "group"), P("dp", "group"), P(), P("dp", "group"))
    return jax.shard_map(
        body, mesh=mesh, in_specs=placed, out_specs=(P("dp", "group"), P("group")), check_vma=False
    )
```

profile of v0, /device:TPU:0, one launch (start us, length us, event | category | flops | bytes accessed | tf_op | source)
XLA Modules:
  0.0 399.3 jit_solution(11375118699398276510)
XLA Ops:
  8.0 4.3 %copy.55 = bf16[6656,256]{0,1:T(8,128)(2,1)S(1)} copy(bf16[6656,256]{1,0:T(8,128)(2,1)} %param.7) | data formatting | bytes 6815744 | tf_op args[3]
  13.8 12.1 %all_gather.7 = bf16[768,256]{1,0:T(8,128)(2,1)} all-gather(bf16[96,256]{1,0:T(8,128)(2,1)S(1)} %copy-done.6), channel_id=1, replica_groups=mesh['dp'=8,'group'=4] {'dp'}, dimensions={0}, use_global_device_ids=true | all-gather | bytes 442368 | tf_op jit(solution)/shard_map/all_gather | solution.py:63
  25.9 0.8 dynamic-slice_multiply_fusion
  26.9 0.9 fusion.33
  27.8 3.7 convert_multiply_fusion.1
  31.5 160.4 %all-gather.2.cloned.1.call-done = bf16[6656,768]{0,1:T(8,128)(2,1)} async-done(((bf16[6656,192]{0,1:T(8,128)(2,1)}), bf16[6656,768]{0,1:T(8,128)(2,1)}) %all-gather.2.cloned.1.call-update) | async-done | bytes 10223632 | tf_op jit(solution)/shard_map/all_gather | solution.py:64
  191.9 8.6 %convert_reduce_fusion = (f32[256]{0:T(256)S(1)}, bf16[6656,256]{0,1:T(8,128)(2,1)}) fusion(bf16[6656,768]{0,1:T(8,128)(2,1)} %all-gather.2.cloned.1.call-done, bf16[768,256]{1,0:T(8,128)(2,1)} %all_gather.7), kind=kOutput, calls=%fused_computation.7 | convolution fusion | flops 2622357248 | bytes 14025728 | tf_op jit(solution)/shard_map/dot_general | solution.py:68
  200.5 13.9 %psum.36 = f32[256]{0:T(256)S(1)} all-reduce(f32[256]{0:T(256)S(1)} %get-tuple-element.19), channel_id=1, replica_groups=mesh['dp'=8,'group'=4] {'dp'}, use_global_device_ids=true, to_apply=%region_2.0 | all-reduce | flops 256 | bytes 2048 | tf_op jit(solution)/shard_map/psum | solution.py:73
  214.5 3.0 convert_subtract_fusion
  217.4 1.7 fusion.56
  219.1 1.8 copy-done
  220.9 0.9 slice-done.3
  221.9 6.9 %fusion.65 = f32[4,64,64]{2,1,0:T(8,128)} fusion(f32[6656,4,64]{0,2,1:T(8,128)S(1)} %bitcast.104, f32[6656,4,64]{0,2,1:T(8,128)S(1)} %bitcast.97), kind=kOutput, calls=%fused_computation.113 | convolution fusion | flops 1308622848 | bytes 13697024 | tf_op jit(solution)/shard_map/tga,tgb->gab/dot_general | solution.py:43
  229.8 49.5 %all-reduce.4.cloned.1.call-done = (f32[4,64,64]{2,1,0:T(8,128)}, f32[4,64,64]{2,1,0:T(8,128)}) async-done(((f32[4,64,64]{2,1,0:T(8,128)}, f32[4,64,64]{2,1,0:T(8,128)}), (f32[4,64,64]{2,1,0:T(8,128)}, f32[4,64,64]{2,1,0:T(8,128)})) %all-reduce.4.cloned.1.call-update) | async-done | bytes 131088 | tf_op jit(solution)/shard_map/psum | solution.py:73
  279.3 1.0 subtract_add_fusion
  280.3 0.8 copy.54
  281.1 1.0 select_reduce_fusion
  282.1 1.2 fusion.10
  286.2 1.3 fusion.17
  287.9 1.3 convolution_add_fusion.16
  295.6 1.0 multiply_reduce_fusion.1
  296.7 8.2 %fusion.52 = f32[4,64,6656]{2,1,0:T(8,128)} fusion(f32[6656,4,64]{0,2,1:T(8,128)S(1)} %bitcast.101, f32[4,64,64]{2,1,0:T(8,128)S(1)} %get-tuple-element.22, f32[4]{0:T(128)S(1)} %get-tuple-element.18), kind=kOutput, calls=%fused_computation.100 | convolution fusion | flops 1308639232 | bytes 13697040 | tf_op jit(solution)/shard_map/tgb,gab->tga/dot_general | solution.py:37
  304.9 8.0 %fusion.54 = f32[4,64,6656]{2,1,0:T(8,128)} fusion(f32[6656,4,64]{0,2,1:T(8,128)S(1)} %bitcast.107, f32[4,64,64]{2,1,0:T(8,128)S(1)} %get-tuple-element.22, f32[4]{0:T(128)S(1)} %get-tuple-element.18), kind=kOutput, calls=%fused_computation.102 | convolution fusion | flops 1308639232 | bytes 13697040 | tf_op jit(solution)/shard_map/tga,gab->tgb/dot_general | solution.py:51
  314.8 1.6 multiply_reduce_fusion
  316.4 1.7 copy.70
  318.1 5.2 %fusion.3 = (f32[256]{0:T(256)}, f32[256]{0:T(256)}) fusion(bf16[6656,256]{0,1:T(8,128)(2,1)S(1)} %copy.55, f32[4,64,6656]{2,1,0:T(8,128)} %fusion.52, f32[256]{0:T(256)} %copy-done.8), kind=kLoop, calls=%fused_computation.9 | loop fusion | flops 10223104 | bytes 10226688 | tf_op jit(solution)/shard_map/reduce_sum | solution.py:41
  324.0 12.8 %all-reduce = (f32[4,64]{1,0:T(4,128)S(1)}, f32[256]{0:T(256)}) all-reduce(f32[4,64]{1,0:T(4,128)S(1)} %reduce_sum.70, f32[256]{0:T(256)} %get-tuple-element.8), channel_id=1, replica_groups=mesh['dp'=8,'group'=4] {'dp'}, use_global_device_ids=true, to_apply=%region_8.9 | all-reduce | flops 512 | bytes 4096 | tf_op jit(solution)/shard_map/psum | solution.py:87
  336.8 1.0 fusion.53
  338.5 10.0 %fusion.1 = bf16[4,64,6656]{2,1,0:T(8,128)(2,1)S(1)} fusion(f32[4,64,6656]{2,1,0:T(8,128)} %fusion.54, f32[6656,4,64]{0,2,1:T(8,128)} %bitcast.98, f32[4,64]{1,0:T(4,128)S(1)} %broadcast_multiply_fusion, f32[4,64,64]{2,1,0:T(8,128)} %get-tuple-element.15, f32[4,64,64]{1,2,0:T(8,128)} %copy.70, f32[4]{0:T(128)S(1)} %negate_add_fusion, ...), kind=kOutput, calls=%fused_computation.2 | convolution fusion | flops 1313832960 | bytes 17179664 | tf_op jit(solution)/shard_map/tgb,gcb->tgc/dot_general | solution.py:52
  348.4 7.6 %convolution_bitcast_fusion = f32[768,256]{0,1:T(8,128)} fusion(bf16[6656,256]{0,1:T(8,128)(2,1)S(1)} %bitcast.109, bf16[6656,768]{0,1:T(8,128)(2,1)} %all-gather.2.cloned.1.call-done), kind=kOutput, calls=%fused_computation.10 | convolution fusion | flops 2617245696 | bytes 14417920 | tf_op jit(solution)/shard_map/dot_general | solution.py:90
  356.1 2.3 copy.90
  358.4 34.4 %reduce-scatter.4.cloned.1.call-done = f32[96,256]{1,0:T(8,128)} async-done(((f32[768,256]{1,0:T(8,128)}), f32[96,256]{1,0:T(8,128)}) %reduce-scatter.4.cloned.1.call-update) | async-done | bytes 98320
  (86 shorter events, 16.2 us)
Async XLA Ops:
  7.2 6.7 %copy-start.6 = (bf16[96,256]{1,0:T(8,128)(2,1)S(1)}, bf16[96,256]{1,0:T(8,128)(2,1)}, u32[]{:S(2)}) copy-start(bf16[96,256]{1,0:T(8,128)(2,1)} %param.5) | copy-start | bytes 147460
  7.2 184.7 %all-gather.2.cloned.1.call-start = ((), (), s32[]{:S(2)}) async-start(), calls=%async_computation.1 | async-start | bytes 12779520 | tf_op jit(solution)/shard_map/all_gather | solution.py:64
  7.9 271.4 %all-reduce.4.cloned.1.call-start = ((), (), s32[]{:S(2)}) async-start(), calls=%async_computation.3 | async-start | bytes 524288 | tf_op jit(solution)/shard_map/psum | solution.py:73
  26.7 1.2 copy-start.8
  214.4 3.0 copy-start.1
  214.4 6.5 %slice-start.2 = ((s8[6815744]{0:T(1024)(128)(4,1)}), s8[4194304]{0:T(1024)(128)(4,1)S(1)}, s32[]{:S(2)}) async-start(s8[6815744]{0:T(1024)(128)(4,1)} %bitcast.102), calls=%async_computation.6 | async-start | bytes 8388608
  214.4 7.4 %slice-start.3 = ((s8[6815744]{0:T(1024)(128)(4,1)}), s8[2621440]{0:T(1024)(128)(4,1)S(1)}, s32[]{:S(2)}) async-start(s8[6815744]{0:T(1024)(128)(4,1)} %bitcast.102), calls=%async_computation.7 | async-start | bytes 5242880
  217.4 3.5 copy-start
  228.8 164.0 %reduce-scatter.4.cloned.1.call-start = ((), (), s32[]{:S(2)}) async-start(), calls=%async_computation.2 | async-start | bytes 884736
  282.1 32.7 %copy-start.7 = (f32[4]{0:T(128)}, f32[4]{0:T(128)S(1)}, u32[]{:S(2)}) copy-start(f32[4]{0:T(128)S(1)} %select_reduce_fusion) | copy-start | bytes 52
  282.1 22.7 %copy-start.9 = (f32[4]{0:T(128)}, f32[4]{0:T(128)S(1)}, u32[]{:S(2)}) copy-start(f32[4]{0:T(128)S(1)} %get-tuple-element.18) | copy-start | bytes 52
  283.4 13.3 %slice-start = ((s8[6815744]{0:T(1024)(128)(4,1)}), s8[4194304]{0:T(1024)(128)(4,1)S(1)}, s32[]{:S(2)}) async-start(s8[6815744]{0:T(1024)(128)(4,1)} %bitcast.99), calls=%async_computation.4 | async-start | bytes 8388608
  283.6 11.5 %copy-start.4 = (f32[4,64,64]{2,1,0:T(8,128)S(1)}, f32[4,64,64]{2,1,0:T(8,128)}, u32[]{:S(2)}) copy-start(f32[4,64,64]{2,1,0:T(8,128)} %get-tuple-element.13) | copy-start | bytes 196612
  289.9 6.7 %slice-start.1 = ((s8[6815744]{0:T(1024)(128)(4,1)}), s8[2621440]{0:T(1024)(128)(4,1)S(1)}, s32[]{:S(2)}) async-start(s8[6815744]{0:T(1024)(128)(4,1)} %bitcast.99), calls=%async_computation.5 | async-start | bytes 5242880
  295.2 9.7 %slice-start.4 = ((s8[6815744]{0:T(1024)(128)(4,1)}), s8[4194304]{0:T(1024)(128)(4,1)S(1)}, s32[]{:S(2)}) async-start(s8[6815744]{0:T(1024)(128)(4,1)} %bitcast.105), calls=%async_computation.8 | async-start | bytes 8388608
  296.6 8.2 %copy-start.2 = (f32[4,64,64]{2,1,0:T(8,128)}, f32[4,64,64]{2,1,0:T(8,128)S(1)}, u32[]{:S(2)}) copy-start(f32[4,64,64]{2,1,0:T(8,128)S(1)} %get-tuple-element.22) | copy-start | bytes 196612
  296.6 8.2 %slice-start.5 = ((s8[6815744]{0:T(1024)(128)(4,1)}), s8[2621440]{0:T(1024)(128)(4,1)S(1)}, s32[]{:S(2)}) async-start(s8[6815744]{0:T(1024)(128)(4,1)} %bitcast.105), calls=%async_computation.9 | async-start | bytes 5242880
  304.9 9.9 %copy-start.5 = (f32[4,64,64]{2,1,0:T(8,128)S(1)}, f32[4,64,64]{2,1,0:T(8,128)}, u32[]{:S(2)}) copy-start(f32[4,64,64]{2,1,0:T(8,128)} %fusion.33) | copy-start | bytes 196612
  316.4 20.4 %copy-start.3 = (f32[4,64,64]{2,1,0:T(8,128)S(1)}, f32[4,64,64]{2,1,0:T(8,128)}, u32[]{:S(2)}) copy-start(f32[4,64,64]{2,1,0:T(8,128)} %copy-done.2) | copy-start | bytes 196612
Sparse Core Ops, SparseCore 0:
  9.5 182.3 all-gather.1
  228.9 50.3 all-reduce.3
  358.5 34.2 reduce-scatter.3
where the time goes:
time: 400 us; the launch traced here: 399 us
  waiting for transfers between devices  245 us (61%)
  matrix products  70.8 us (18%)
  blocking collectives  38.8 us (10%)
  other arithmetic  15.4 us (4%)
  local copies, waits for them, and re-layouts  14.8 us (4%)
  between operations  14.2 us (4%)
    all_gather x1, waiting for transfers between devices, body(): full_patches = lax.all_gather(patches, 'group', axis=1, tiled=True)  160 us
    psum x1, waiting for transfers between devices, body(): lax.psum((jnp.sum(features, axis=0), group_products(raw_grouped)), 'dp')  49.5 us
    unnamed x4, waiting for transfers between devices  35.1 us
    dot_general x40, matrix products, matmul_batch(): return jnp.einsum('gij,gjk->gik', left, right, precision=highest)  18.9 us
    psum x1, blocking collectives, body(): lax.psum((jnp.sum(features, axis=0), group_products(raw_grouped)), 'dp')  13.9 us
    psum x1, blocking collectives, body(): summed = lax.psum((partials[0], partials[1], partials[2]), 'dp')  12.8 us
    all_gather x1, blocking collectives, body(): weights = lax.all_gather(embed_weight, 'dp', axis=0, tiled=True)  12.1 us
    dot_general x1, matrix products, finish_backward(): through = jnp.einsum('tgb,gcb->tgc', grouped, symmetric, precision=highest)  9.97 us
  transfers between devices with their start and end apart: 3, of which 3 were waited for; matrix products, arithmetic and copies ran while one was open for 3% of the time, Pallas kernels for 0%

commit v1 on v0

v1 whole, which is shorter than its diff:
```python
import math

import jax
import jax.numpy as jnp
from jax import lax
from jax.sharding import PartitionSpec as P

GW = 64
ITERS = 5


EPSILON = 1e-05
highest = lax.Precision.HIGHEST


def matmul_batch(left, right):
    return jnp.einsum("gij,gjk->gik", left, right, precision=highest)


def whiten_matrix(covariance):
    width = covariance.shape[-1]
    traces = jnp.trace(covariance, axis1=1, axis2=2)
    normed = covariance / traces[:, None, None]
    iterate = jnp.broadcast_to(jnp.eye(width, dtype=jnp.float32), covariance.shape)
    for counter in range(ITERS):
        cubed = matmul_batch(matmul_batch(iterate, iterate), iterate)
        iterate = 1.5 * iterate - 0.5 * matmul_batch(cubed, normed)
    return iterate / jnp.sqrt(traces)[:, None, None]


def block_diagonals(square):
    width = square.shape[0]
    groups = width // GW
    blocks = square.reshape(groups, GW, groups, GW)
    return jnp.stack([blocks[g, :, g, :] for g in range(groups)])


def contract_tokens(left, right):
    return lax.dot_general(
        left, right, (((0,), (0,)), ((), ())), preferred_element_type=jnp.float32
    )


def body(patches, embed_weight, channel_gain, cotangent):
    tok_rows = patches.shape[0]
    total_tokens = tok_rows * lax.axis_size("dp")
    loss_scale = 1.0 / math.sqrt(total_tokens)
    identity = jnp.eye(GW, dtype=jnp.float32)
    width_here = embed_weight.shape[1]
    weights = lax.all_gather(embed_weight, "dp", axis=0, tiled=True)
    full_patches = lax.all_gather(patches, "group", axis=1, tiled=True)
    gain_here = lax.dynamic_slice_in_dim(
        channel_gain, lax.axis_index("group") * width_here, width_here
    )
    embedded = jnp.dot(full_patches, weights, preferred_element_type=jnp.float32).astype(
        jnp.bfloat16
    )
    both = jnp.concatenate([embedded, cotangent], axis=1)
    stats = contract_tokens(embedded, both)
    raw_products = block_diagonals(stats[:, :width_here])
    cross = jnp.swapaxes(block_diagonals(stats[:, width_here:]), 1, 2)
    sums = jnp.sum(both.astype(jnp.float32), axis=0)
    raw_products, cross, sums = lax.psum((raw_products, cross, sums), "dp")
    patch_products = jnp.concatenate(
        [
            contract_tokens(full_patches, both),
            jnp.broadcast_to(
                jnp.sum(full_patches.astype(jnp.float32), axis=0)[:, None],
                (full_patches.shape[1], 128),
            ),
        ],
        axis=1,
    )
    patch_products = lax.psum_scatter(patch_products, "dp", scatter_dimension=0, tiled=True)
    return finish(
        raw_products, cross, sums, patch_products, gain_here, loss_scale, total_tokens, identity
    )


def finish(raw_products, cross, sums, patch_products, gain_here, loss_scale, total_tokens, identity):
    width_here = gain_here.shape[0]
    mean_groups = (sums[:width_here] / total_tokens).reshape(-1, GW)
    cot_sums = sums[width_here:].reshape(-1, GW)
    covariance = (
        raw_products / total_tokens
        - jnp.einsum("ga,gb->gab", mean_groups, mean_groups, precision=highest)
        + EPSILON * identity
    )
    whitener, pullback = jax.vjp(whiten_matrix, covariance)
    cross = loss_scale * (
        cross - jnp.einsum("ga,gb->gab", cot_sums, mean_groups, precision=highest)
    )
    gain_grad = jnp.sum(cross * whitener, axis=2).reshape(-1)
    scale = loss_scale * gain_here
    (grad_cov,) = pullback(cross * gain_here.reshape(-1, GW)[:, :, None])
    symmetric = (grad_cov + jnp.swapaxes(grad_cov, 1, 2)) / total_tokens
    patch_sums = patch_products[:, 2 * width_here : 2 * width_here + 1]
    rows = patch_products.shape[0]
    feat_part = patch_products[:, :width_here] - patch_sums * mean_groups.reshape(-1)
    cot_part = scale * (
        patch_products[:, width_here : 2 * width_here]
        - patch_sums * (cot_sums.reshape(-1) / total_tokens)
    )
    weight_grad = jnp.einsum(
        "rga,gab->rgb", cot_part.reshape(rows, -1, GW), whitener, precision=highest
    ) + jnp.einsum("rgb,gcb->rgc", feat_part.reshape(rows, -1, GW), symmetric, precision=highest)
    return (weight_grad.reshape(rows, -1), gain_grad)


def solution(mesh):
    placed = (P("dp", "group"), P("dp", "group"), P(), P("dp", "group"))
    return jax.shard_map(
        body, mesh=mesh, in_specs=placed, out_specs=(P("dp", "group"), P("group")), check_vma=False
    )
```

time: 400 us -> 334 us (0.83)
  matrix products: 70.8 us -> 35.9 us
  waiting for transfers between devices: 245 us -> 222 us
  blocking collectives: 38.8 us -> 26.5 us
  local copies, waits for them, and re-layouts: 14.8 us -> 21.9 us
    dot_general x7 -> x4, matrix products: 43.3 us -> 13.8 us  [the longest x2 13.2 us: contract_tokens(): lax.dot_general(left, right, (((0,), (0,)), ((), ())), preferred_element_...]
    psum x1, waiting for transfers between devices: 49.5 us -> 32.1 us  [body(): raw_products, cross, sums = lax.psum((raw_products, cross, sums), 'dp')]
    psum x2 -> x1, blocking collectives: 26.7 us -> 14.5 us  [body(): raw_products, cross, sums = lax.psum((raw_products, cross, sums), 'dp')]
    unnamed x4, waiting for transfers between devices: 35.1 us -> 26.4 us
    slice x0 -> x5, local copies, waits for them, and re-layouts: none -> 6.69 us  [the longest x2 3.09 us: block_diagonals(): return jnp.stack([blocks[g, :, g, :] for g in range(groups)])]
    reshape x1 -> x4, local copies, waits for them, and re-layouts: 0.66 us -> 4.67 us  [the longest x2 3.94 us: block_diagonals(): blocks = square.reshape(groups, GW, groups, GW)]
    unnamed x34 -> x28, local copies, waits for them, and re-layouts: 9.43 us -> 8.1 us
  transfers between devices with their start and end apart: 3 -> 3, of which waited for: 3 -> 3; matrix products, arithmetic and copies ran while one was open for 3% -> 13% of each run, Pallas kernels for 0% -> 0%
where the time goes in v1:
time: 334 us; the launch traced here: 333 us
  waiting for transfers between devices  222 us (66%)
  matrix products  35.9 us (11%)
  blocking collectives  26.5 us (8%)
  local copies, waits for them, and re-layouts  21.9 us (7%)
  between operations  14.3 us (4%)
  other arithmetic  12.3 us (4%)
    all_gather x1, waiting for transfers between devices, body(): full_patches = lax.all_gather(patches, 'group', axis=1, tiled=True)  164 us
    psum x1, waiting for transfers between devices, body(): raw_products, cross, sums = lax.psum((raw_products, cross, sums), 'dp')  32.1 us
    unnamed x4, waiting for transfers between devices  26.4 us
    dot_general x40, matrix products, matmul_batch(): return jnp.einsum('gij,gjk->gik', left, right, precision=highest)  15.4 us
    psum x1, blocking collectives, body(): raw_products, cross, sums = lax.psum((raw_products, cross, sums), 'dp')  14.5 us
    dot_general x2, matrix products, contract_tokens(): lax.dot_general(left, right, (((0,), (0,)), ((), ())), preferred_element_...  13.2 us
    all_gather x1, blocking collectives, body(): weights = lax.all_gather(embed_weight, 'dp', axis=0, tiled=True)  12.1 us
    unnamed x28, local copies, waits for them, and re-layouts  8.1 us
  transfers between devices with their start and end apart: 3, of which 3 were waited for; matrix products, arithmetic and copies ran while one was open for 13% of the time, Pallas kernels for 0%

profile of v1, /device:TPU:0, one launch (start us, length us, event | category | flops | bytes accessed | tf_op | source)
XLA Modules:
  0.0 333.1 jit_solution(15278227765945811234)
XLA Ops:
  7.2 0.7 all-gather.2.cloned.1.call-update
  8.0 4.3 %copy.76 = bf16[6656,256]{0,1:T(8,128)(2,1)S(1)} copy(bf16[6656,256]{1,0:T(8,128)(2,1)} %param.7) | data formatting | bytes 6815744 | tf_op args[3]
  12.3 0.7 copy.82
  13.0 0.8 dynamic-slice_multiply_fusion
  13.8 0.6 copy-done.5
  14.4 0.7 mul.188
  15.0 0.7 copy.75
  15.7 12.1 %all_gather.7 = bf16[768,256]{1,0:T(8,128)(2,1)} all-gather(bf16[96,256]{1,0:T(8,128)(2,1)S(1)} %copy-done.2), channel_id=1, replica_groups=mesh['dp'=8,'group'=4] {'dp'}, dimensions={0}, use_global_device_ids=true | all-gather | bytes 442368 | tf_op jit(solution)/shard_map/all_gather | solution.py:50
  28.4 163.6 %all-gather.2.cloned.1.call-done = bf16[6656,768]{0,1:T(8,128)(2,1)} async-done(((bf16[6656,192]{0,1:T(8,128)(2,1)}), bf16[6656,768]{0,1:T(8,128)(2,1)}) %all-gather.2.cloned.1.call-update) | async-done | bytes 10223632 | tf_op jit(solution)/shard_map/all_gather | solution.py:51
  191.9 6.8 %convolution_convert_fusion = bf16[6656,256]{0,1:T(8,128)(2,1)S(1)} fusion(bf16[6656,768]{0,1:T(8,128)(2,1)} %all-gather.2.cloned.1.call-done, bf16[768,256]{1,0:T(8,128)(2,1)} %all_gather.7), kind=kOutput, calls=%fused_computation.2 | convolution fusion | flops 2618949632 | bytes 14024704 | tf_op jit(solution)/shard_map/dot_general | solution.py:55
  198.7 1.7 convert_reduce_fusion.1
  200.5 2.7 fusion.1
  203.2 14.5 %psum.22 = f32[512]{0:T(512)} all-reduce(f32[512]{0:T(512)} %convert_reduce_fusion.1), channel_id=1, replica_groups=mesh['dp'=8,'group'=4] {'dp'}, use_global_device_ids=true, to_apply=%region_2.0 | all-reduce | flops 512 | bytes 4096 | tf_op jit(solution)/shard_map/psum | solution.py:63
  217.7 1.4 fusion.58
  219.1 1.8 fusion.55
  220.9 2.0 reshape.83
  222.9 1.9 fusion.56
  224.7 2.0 reshape.85
  226.7 1.2 fusion.54
  227.9 1.5 pad_maximum_fusion.6
  229.5 5.4 %convert_reduce_fusion = f32[768]{0:T(1024)S(1)} fusion(bf16[6656,768]{0,1:T(8,128)(2,1)} %all-gather.2.cloned.1.call-done), kind=kLoop, calls=%fused_computation | loop fusion | flops 10222848 | bytes 10226688 | tf_op jit(solution)/shard_map/reduce_sum | solution.py:68
  234.9 10.4 %fusion.2 = f32[768,512]{0,1:T(8,128)S(1)} fusion(bf16[6656,768]{0,1:T(8,128)(2,1)} %all-gather.2.cloned.1.call-done, bf16[6656,256]{0,1:T(8,128)(2,1)S(1)} %copy.76, bf16[6656,256]{0,1:T(8,128)(2,1)} %copy-done), kind=kOutput, calls=%fused_computation.7 | convolution fusion | flops 5248122880 | bytes 18612224 | tf_op jit(solution)/shard_map/dot_general | solution.py:39
  245.6 2.0 copy.198
  247.8 32.1 %all-reduce.3.cloned.1.call-done = (f32[4,64,64]{2,1,0:T(8,128)}, f32[4,64,64]{1,2,0:T(8,128)}) async-done(((f32[4,64,64]{2,1,0:T(8,128)}, f32[4,64,64]{1,2,0:T(8,128)}), (f32[4,64,64]{2,1,0:T(8,128)}, f32[4,64,64]{1,2,0:T(8,128)})) %all-reduce.3.cloned.1.call-update) | async-done | bytes 131088 | tf_op jit(solution)/shard_map/psum | solution.py:63
  280.0 1.0 broadcast_multiply_fusion
  285.6 1.4 fusion.16
  296.1 0.5 multiply_reduce_fusion
  296.6 0.6 reshape.89
  297.3 25.6 %reduce-scatter.4.cloned.1.call-done = f32[96,640]{1,0:T(8,128)} async-done(((f32[768,640]{1,0:T(8,128)}), f32[96,640]{1,0:T(8,128)}) %reduce-scatter.4.cloned.1.call-update) | async-done | bytes 245776
  322.9 1.0 fusion.57
  324.0 0.8 slice.82
  325.8 0.7 copy.143
  (85 shorter events, 15.7 us)
Async XLA Ops:
  7.2 8.6 %copy-start.2 = (bf16[96,256]{1,0:T(8,128)(2,1)S(1)}, bf16[96,256]{1,0:T(8,128)(2,1)}, u32[]{:S(2)}) copy-start(bf16[96,256]{1,0:T(8,128)(2,1)} %param.5) | copy-start | bytes 147460
  7.2 184.7 %all-gather.2.cloned.1.call-start = ((), (), s32[]{:S(2)}) async-start(), calls=%async_computation.1 | async-start | bytes 12779520 | tf_op jit(solution)/shard_map/all_gather | solution.py:51
  7.9 272.0 %all-reduce.3.cloned.1.call-start = ((), (), s32[]{:S(2)}) async-start(), calls=%async_computation.3 | async-start | bytes 524288 | tf_op jit(solution)/shard_map/psum | solution.py:63
  13.8 0.6 copy-start.5
  198.7 1.8 copy-start
  229.5 93.4 %reduce-scatter.4.cloned.1.call-start = ((), (), s32[]{:S(2)}) async-start(), calls=%async_computation.2 | async-start | bytes 2211840
  245.4 2.3 copy-start.8
  245.4 2.3 copy-start.4
  245.4 35.6 %copy-start.1 = (f32[64,64]{0,1:T(8,128)S(1)}, f32[64,64]{0,1:T(8,128)}, u32[]{:S(2)}) copy-start(f32[64,64]{0,1:T(8,128)} %copy.82) | copy-start | bytes 49156
  245.4 35.9 %copy-start.3 = (f32[64,64]{0,1:T(8,128)S(1)}, f32[64,64]{0,1:T(8,128)}, u32[]{:S(2)}) copy-start(f32[64,64]{0,1:T(8,128)} %copy.75) | copy-start | bytes 49156
  245.6 40.0 %copy-start.9 = (f32[4,64]{1,0:T(4,128)S(1)}, f32[4,64]{1,0:T(4,128)}, u32[]{:S(2)}) copy-start(f32[4,64]{1,0:T(4,128)} %mul.188) | copy-start | bytes 3076
  280.0 7.4 %copy-start.10 = (f32[4,64,64]{1,2,0:T(8,128)S(1)}, f32[4,64,64]{1,2,0:T(8,128)}, u32[]{:S(2)}) copy-start(f32[4,64,64]{1,2,0:T(8,128)} %get-tuple-element.9) | copy-start | bytes 196612
  288.1 36.9 %copy-start.6 = (f32[256]{0:T(256)S(1)}, f32[256]{0:T(256)}, u32[]{:S(2)}) copy-start(f32[256]{0:T(256)} %copy-done.5) | copy-start | bytes 3076
  288.1 36.9 %copy-start.7 = (f32[256]{0:T(256)S(1)}, f32[256]{0:T(256)}, u32[]{:S(2)}) copy-start(f32[256]{0:T(256)} %get-tuple-element.25) | copy-start | bytes 3076
Sparse Core Ops, SparseCore 0:
  9.5 182.3 all-gather.1
  229.6 50.2 all-reduce.2
  283.4 39.5 reduce-scatter.3

commit v2 on v1

--- a/solution.py
+++ b/solution.py
@@ -1,8 +1,11 @@
+import functools
 import math
 
 import jax
 import jax.numpy as jnp
 from jax import lax
+from jax.experimental import pallas as pl
+from jax.experimental.pallas import tpu as pltpu
 from jax.sharding import PartitionSpec as P
 
 GW = 64
@@ -35,10 +38,229 @@
     return jnp.stack([blocks[g, :, g, :] for g in range(groups)])
 
 
-def contract_tokens(left, right):
-    return lax.dot_general(
-        left, right, (((0,), (0,)), ((), ())), preferred_element_type=jnp.float32
-    )
+MESH = pl.DeviceIdType.MESH
+LEAD = 2
+
+
+def window_of(part, depth):
+    start = part * depth // 128 * 128
+    stop = -(-(part + 1) * depth // 128) * 128
+    return start, stop - start, part * depth - start
+
+
+def token_kernel(
+    n, ndp, parts, depth, chunk,
+    x_hbm, cot_hbm, w_hbm,
+    out_ref, stats_ref,
+    held, cot, weights, padded, totals, patch_sums, bank,
+    send_right, recv_right, send_left, recv_left, w_send, w_recv, local_sem,
+):
+    me = lax.axis_index("group")
+    mine = lax.axis_index("dp")
+    right, left = lax.rem(me + 1, n), lax.rem(me + n - 1, n)
+    rows = x_hbm.shape[0]
+    chunks = rows // chunk
+    width = cot.shape[1]
+    hops = n // 2
+    slab = w_hbm.shape[0]
+
+    own_x = pltpu.make_async_copy(x_hbm, held.at[0], local_sem.at[0])
+    own_cot = pltpu.make_async_copy(cot_hbm, cot, local_sem.at[1])
+    own_w = pltpu.make_async_copy(w_hbm, weights.at[mine], local_sem.at[2])
+    own_x.start()
+    own_cot.start()
+    own_w.start()
+
+    barrier = pltpu.get_barrier_semaphore()
+    for step in range(1, ndp):
+        pl.semaphore_signal(
+            barrier, inc=1, device_id={"dp": lax.rem(mine + step, ndp)}, device_id_type=MESH
+        )
+    for neighbour in (left, right):
+        pl.semaphore_signal(barrier, inc=1, device_id={"group": neighbour}, device_id_type=MESH)
+    pl.semaphore_wait(barrier, ndp + 1)
+
+    def w_copy(step):
+        return pltpu.make_async_remote_copy(
+            src_ref=w_hbm,
+            dst_ref=weights.at[mine],
+            send_sem=w_send.at[step],
+            recv_sem=w_recv.at[step],
+            device_id={"dp": lax.rem(mine + step, ndp)},
+            device_id_type=MESH,
+        )
+
+    def x_copy(hop, piece, to_right):
+        start, size = pl.multiple_of(piece * chunk, chunk), chunk
+        if n % 2 == 0 and hop == hops:
+            size = chunk // 2
+            if not to_right:
+                start = start + size
+        span = pl.ds(pl.multiple_of(start, size), size)
+        source = x_hbm.at[span] if hop == 1 else held.at[hop - 1 if to_right else n - hop + 1, span]
+        send, recv = (send_right, recv_right) if to_right else (send_left, recv_left)
+        return pltpu.make_async_remote_copy(
+            src_ref=source,
+            dst_ref=held.at[hop if to_right else n - hop, span],
+            send_sem=send.at[hop - 1, piece],
+            recv_sem=recv.at[hop - 1, piece],
+            device_id={"group": right if to_right else left},
+            device_id_type=MESH,
+        )
+
+    for step in range(1, ndp):
+        w_copy(step).start()
+    for piece in range(min(LEAD, chunks)):
+        for to_right in (True, False):
+            x_copy(1, piece, to_right).start()
+
+    totals[...] = jnp.zeros_like(totals)
+    patch_sums[...] = jnp.zeros_like(patch_sums)
+    stats_ref[...] = jnp.zeros_like(stats_ref)
+    padded[...] = jnp.zeros_like(padded)
+    own_w.wait()
+    for step in range(1, ndp):
+        w_copy(step).wait()
+    per = depth // slab
+    for j in range(n):
+        for part in range(parts):
+            offset = window_of(part, depth)[2]
+            for k in range(per):
+                padded[j, part, offset + k * slab : offset + (k + 1) * slab, :] = weights[
+                    j * per + k
+                ]
+    own_x.wait()
+    own_cot.wait()
+    ones = jnp.ones((16, chunk), jnp.bfloat16)
+
+    def compute(piece):
+        span = pl.ds(pl.multiple_of(piece * chunk, chunk), chunk)
+        for part in range(parts):
+            start, size, _ = window_of(part, depth)
+            embedded = jnp.zeros((chunk, width), jnp.float32)
+            for slot in range(n):
+                origin = lax.rem(me - slot + n, n)
+                embedded += jnp.dot(
+                    held[slot, span, start : start + size],
+                    padded[origin, part, :size, :],
+                    preferred_element_type=jnp.float32,
+                )
+            tokens = pl.ds(pl.multiple_of(part * rows + piece * chunk, chunk), chunk)
+            bank[:, :width] = embedded.astype(jnp.bfloat16)
+            bank[:, width:] = cot[tokens, :]
+            both = bank[...]
+            flipped = both.T
+            stats_ref[:width, :] += jnp.dot(
+                flipped[:width], both, preferred_element_type=jnp.float32
+            )
+            stats_ref[width:, :] += jnp.dot(ones, both, preferred_element_type=jnp.float32)[:8]
+            for slot in range(n):
+                totals[slot, part, :, :size] += jnp.dot(
+                    flipped,
+                    held[slot, span, start : start + size],
+                    preferred_element_type=jnp.float32,
+                )
+        for slot in range(n):
+            patch_sums[slot] += jnp.dot(
+                ones, held[slot, span, :], preferred_element_type=jnp.float32
+            )[:8]
+
+    def arrive(hop, piece):
+        for to_right in (True, False):
+            x_copy(hop, piece, to_right).wait()
+
+    @pl.loop(0, chunks + LEAD * (hops - 1))
+    def _(step):
+        @pl.when(step + LEAD < chunks)
+        def _():
+            for to_right in (True, False):
+                x_copy(1, step + LEAD, to_right).start()
+
+        for hop in range(1, hops):
+            piece = step - LEAD * (hop - 1)
+
+            @pl.when((piece >= 0) & (piece < chunks))
+            def _():
+                for to_right in (True, False):
+                    x_copy(hop, piece, to_right).wait_recv()
+                    x_copy(hop + 1, piece, to_right).start()
+
+        piece = step - LEAD * (hops - 1)
+
+        @pl.when(piece >= 0)
+        def _():
+            for to_right in (True, False):
+                x_copy(hops, piece, to_right).wait_recv()
+            compute(piece)
+
+    @pl.loop(0, chunks)
+    def _(piece):
+        for hop in range(1, hops + 1):
+            for to_right in (True, False):
+                x_copy(hop, piece, to_right).wait_send()
+
+    for slot in range(n):
+        origin = lax.rem(me - slot + n, n)
+        base = pl.multiple_of(origin * depth, 8)
+        gathered = None
+        for part in range(parts):
+            start, size, offset = window_of(part, depth)
+            block = totals[slot, part, :, :size].T[offset : offset + depth]
+            gathered = block if gathered is None else gathered + block
+        out_ref[pl.ds(base, depth), : 2 * width] = gathered
+        added = None
+        for part in range(parts):
+            start, size, offset = window_of(part, depth)
+            line = jnp.broadcast_to(patch_sums[slot, :1, start : start + size], (128, size)).T
+            line = line[offset : offset + depth]
+            added = line if added is None else added + line
+        out_ref[pl.ds(base, depth), 2 * width :] = added
+
+
+def token_products(patches, embed_weight, cotangent):
+    n, ndp = lax.axis_size("group"), lax.axis_size("dp")
+    tok_rows, depth = patches.shape
+    width = embed_weight.shape[1]
+    parts = 128 // math.gcd(depth, 128)
+    rows = tok_rows // parts
+    packed = jnp.concatenate(
+        [patches[q * rows : (q + 1) * rows] for q in range(parts)], axis=1
+    )
+    chunk = 256
+    while rows % chunk:
+        chunk //= 2
+    chunks = rows // chunk
+    hops = n // 2
+    lanes = parts * depth
+    window = max(window_of(q, depth)[1] for q in range(parts))
+    anywhere = pl.BlockSpec(memory_space=pl.ANY)
+    in_vmem = pl.BlockSpec(memory_space=pltpu.VMEM)
+    ring = pltpu.SemaphoreType.DMA((hops, chunks))
+    return pl.pallas_call(
+        functools.partial(token_kernel, n, ndp, parts, depth, chunk),
+        out_shape=(
+            jax.ShapeDtypeStruct((n * depth, 2 * width + 128), jnp.float32),
+            jax.ShapeDtypeStruct((width + 8, 2 * width), jnp.float32),
+        ),
+        in_specs=[anywhere] * 3,
+        out_specs=(in_vmem, in_vmem),
+        scratch_shapes=[
+            pltpu.VMEM((n, rows, lanes), jnp.bfloat16),
+            pltpu.VMEM((tok_rows, width), jnp.bfloat16),
+            pltpu.VMEM((ndp,) + embed_weight.shape, jnp.bfloat16),
+            pltpu.VMEM((n, parts, window, width), jnp.bfloat16),
+            pltpu.VMEM((n, parts, 2 * width, window), jnp.float32),
+            pltpu.VMEM((n, 8, lanes), jnp.float32),
+            pltpu.VMEM((chunk, 2 * width), jnp.bfloat16),
+            ring, ring, ring, ring,
+            pltpu.SemaphoreType.DMA((ndp,)),
+            pltpu.SemaphoreType.DMA((ndp,)),
+            pltpu.SemaphoreType.DMA((3,)),
+        ],
+        compiler_params=pltpu.CompilerParams(
+            collective_id=0, has_side_effects=True, vmem_limit_bytes=60 << 20
+        ),
+    )(packed, cotangent, embed_weight)
 
 
 def body(patches, embed_weight, channel_gain, cotangent):
@@ -47,30 +269,14 @@
     loss_scale = 1.0 / math.sqrt(total_tokens)
     identity = jnp.eye(GW, dtype=jnp.float32)
     width_here = embed_weight.shape[1]
-    weights = lax.all_gather(embed_weight, "dp", axis=0, tiled=True)
-    full_patches = lax.all_gather(patches, "group", axis=1, tiled=True)
     gain_here = lax.dynamic_slice_in_dim(
         channel_gain, lax.axis_index("group") * width_here, width_here
     )
-    embedded = jnp.dot(full_patches, weights, preferred_element_type=jnp.float32).astype(
-        jnp.bfloat16
-    )
-    both = jnp.concatenate([embedded, cotangent], axis=1)
-    stats = contract_tokens(embedded, both)
-    raw_products = block_diagonals(stats[:, :width_here])
-    cross = jnp.swapaxes(block_diagonals(stats[:, width_here:]), 1, 2)
-    sums = jnp.sum(both.astype(jnp.float32), axis=0)
+    patch_products, stats = token_products(patches, embed_weight, cotangent)
+    raw_products = block_diagonals(stats[:width_here, :width_here])
+    cross = jnp.swapaxes(block_diagonals(stats[:width_here, width_here:]), 1, 2)
+    sums = stats[width_here]
     raw_products, cross, sums = lax.psum((raw_products, cross, sums), "dp")
-    patch_products = jnp.concatenate(
-        [
-            contract_tokens(full_patches, both),
-            jnp.broadcast_to(
-                jnp.sum(full_patches.astype(jnp.float32), axis=0)[:, None],
-                (full_patches.shape[1], 128),
-            ),
-        ],
-        axis=1,
-    )
     patch_products = lax.psum_scatter(patch_products, "dp", scatter_dimension=0, tiled=True)
     return finish(
         raw_products, cross, sums, patch_products, gain_here, loss_scale, total_tokens, identity

time: 334 us -> 304 us (0.910)
  Pallas kernels: 0 us -> 179 us
  waiting for transfers between devices: 222 us -> 65.7 us
  matrix products: 35.9 us -> 15.1 us
  blocking collectives: 26.5 us -> 12.1 us
  local copies, waits for them, and re-layouts: 21.9 us -> 11.1 us
  other arithmetic: 12.3 us -> 6.14 us
    pallas_call x0 -> x1, Pallas kernels: none -> 179 us  [token_products(): pl.pallas_call(functools.partial(token_kernel, n, ndp, parts, depth, chun...]
    all_gather x1 -> x0, waiting for transfers between devices: 164 us -> none  [body(): full_patches = lax.all_gather(patches, 'group', axis=1, tiled=True)]
    reduce_scatter x0 -> x1, waiting for transfers between devices: none -> 26.6 us  [body(): lax.psum_scatter(patch_products, 'dp', scatter_dimension=0, tiled=True)]
    unnamed x4 -> x2, waiting for transfers between devices: 26.4 us -> 0.71 us
    dot_general x3 -> x0, matrix products: 19.9 us -> none  [the longest x2 13.2 us: contract_tokens(): lax.dot_general(left, right, (((0,), (0,)), ((), ())), preferred_element_...]
    all_gather x1 -> x0, blocking collectives: 12.1 us -> none  [body(): weights = lax.all_gather(embed_weight, 'dp', axis=0, tiled=True)]
    reduce_sum x2 -> x0, other arithmetic: 7.1 us -> none  [the longest x1 5.41 us: body(): jnp.sum(full_patches.astype(jnp.float32), axis=0)[:, None]]
    psum x1, waiting for transfers between devices: 32.1 us -> 38.4 us  [body(): raw_products, cross, sums = lax.psum((raw_products, cross, sums), 'dp')]
  transfers between devices with their start and end apart: 3 -> 2, of which waited for: 3 -> 2; matrix products, arithmetic and copies ran while one was open for 13% -> 6% of each run, Pallas kernels for 0% -> 0%
where the time goes in v2:
time: 304 us; the launch traced here: 303 us
  Pallas kernels  179 us (59%)
  waiting for transfers between devices  65.7 us (22%)
  matrix products  15.1 us (5%)
  between operations  14.5 us (5%)
  blocking collectives  12.1 us (4%)
  local copies, waits for them, and re-layouts  11.1 us (4%)
  other arithmetic  6.14 us (2%)
    pallas_call x1, Pallas kernels, token_products(): pl.pallas_call(functools.partial(token_kernel, n, ndp, parts, depth, chun...  179 us
    psum x1, waiting for transfers between devices, body(): raw_products, cross, sums = lax.psum((raw_products, cross, sums), 'dp')  38.4 us
    reduce_scatter x1, waiting for transfers between devices, body(): lax.psum_scatter(patch_products, 'dp', scatter_dimension=0, tiled=True)  26.6 us
    dot_general x40, matrix products, matmul_batch(): return jnp.einsum('gij,gjk->gik', left, right, precision=highest)  14.5 us
    psum x1, blocking collectives, body(): raw_products, cross, sums = lax.psum((raw_products, cross, sums), 'dp')  12.1 us
  transfers between devices with their start and end apart: 2, of which 2 were waited for; matrix products, arithmetic and copies ran while one was open for 6% of the time, Pallas kernels for 0%

profile of v2, /device:TPU:0, one launch (start us, length us, event | category | flops | bytes accessed | tf_op | source)
XLA Modules:
  0.0 303.2 jit_solution(589290917177245613)
XLA Ops:
  7.2 2.9 fusion.50
  10.1 0.7 copy.204
  10.9 1.7 copy.205
  12.6 2.4 pad_maximum_fusion.x_hbm
  15.0 178.6 %shard_map.59 = (f32[768,640]{1,0:T(8,128)}, f32[264,512]{1,0:T(8,128)}) custom-call(bf16[3328,384]{1,0:T(8,128)(2,1)} %pad_maximum_fusion.x_hbm, bf16[6656,256]{1,0:T(8,128)(2,1)} %cot_hbm.1, bf16[96,256]{1,0:T(8,128)(2,1)} %w_hbm.1), custom_call_target="tpu_custom_call" | custom-call | tf_op jit(solution)/shard_map/pallas_call | solution.py:239
  193.6 1.1 fusion.51
  195.4 0.7 pad_maximum_fusion.1
  196.2 0.7 reduce-scatter.2.cloned.1.call-update
  196.9 0.7 slice.77
  197.7 12.1 %psum.22 = f32[512]{0:T(512)S(1)} all-reduce(f32[512]{0:T(512)S(1)} %bitcast.112), channel_id=1, replica_groups=mesh['dp'=8,'group'=4] {'dp'}, use_global_device_ids=true, to_apply=%region_1.0 | all-reduce | flops 512 | bytes 4096 | tf_op jit(solution)/shard_map/psum | solution.py:279
  209.9 0.8 dynamic-slice_multiply_fusion
  211.4 38.4 %all-reduce.3.cloned.1.call-done = (f32[4,64,64]{2,1,0:T(8,128)}, f32[4,64,64]{1,2,0:T(8,128)}) async-done(((f32[4,64,64]{2,1,0:T(8,128)}, f32[4,64,64]{1,2,0:T(8,128)}), (f32[4,64,64]{2,1,0:T(8,128)}, f32[4,64,64]{1,2,0:T(8,128)})) %all-reduce.3.cloned.1.call-update) | async-done | bytes 131088 | tf_op jit(solution)/shard_map/psum | solution.py:279
  249.9 0.9 broadcast_multiply_fusion
  251.3 0.4 fusion.6
  252.4 0.4 fusion.5
  253.6 0.4 fusion.4
  254.7 0.4 fusion.3
  255.5 0.5 fusion.13
  256.7 0.4 convolution_add_fusion.15
  257.1 0.4 convolution_add_fusion.14
  257.5 0.4 fusion.15
  259.0 0.4 convolution_add_fusion.10
  259.4 0.4 fusion.16
  261.6 0.4 fusion.17
  263.0 0.4 convolution_add_fusion.3
  263.4 0.4 fusion.1
  265.1 0.5 multiply_reduce_fusion
  265.6 0.6 reshape.88
  266.3 26.6 %reduce-scatter.2.cloned.1.call-done = f32[96,640]{1,0:T(8,128)} async-done(((f32[768,640]{1,0:T(8,128)}), f32[96,640]{1,0:T(8,128)}) %reduce-scatter.2.cloned.1.call-update) | async-done | bytes 245776 | tf_op jit(solution)/shard_map/reduce_scatter | solution.py:280
  292.9 0.9 slice_reduce_fusion
  293.8 1.0 slice_subtract_fusion
  295.7 0.7 copy.149
  (56 shorter events, 11.3 us)
Async XLA Ops:
  7.2 242.7 %all-reduce.3.cloned.1.call-start = ((), (), s32[]{:S(2)}) async-start(), calls=%async_computation.2 | async-start | bytes 524288 | tf_op jit(solution)/shard_map/psum | solution.py:279
  196.2 96.7 %reduce-scatter.2.cloned.1.call-start = ((), (), s32[]{:S(2)}) async-start(), calls=%async_computation.1 | async-start | bytes 2211840 | tf_op jit(solution)/shard_map/reduce_scatter | solution.py:280
  251.1 4.4 %copy-start = (f32[4,64,64]{1,2,0:T(8,128)S(1)}, f32[4,64,64]{1,2,0:T(8,128)}, u32[]{:S(2)}) copy-start(f32[4,64,64]{1,2,0:T(8,128)} %get-tuple-element.13) | copy-start | bytes 196612
Sparse Core Ops, SparseCore 0:
  196.3 53.5 all-reduce.2
  253.3 39.5 reduce-scatter.1

commit v3 on v2

--- a/solution.py
+++ b/solution.py
@@ -31,13 +31,6 @@
     return iterate / jnp.sqrt(traces)[:, None, None]
 
 
-def block_diagonals(square):
-    width = square.shape[0]
-    groups = width // GW
-    blocks = square.reshape(groups, GW, groups, GW)
-    return jnp.stack([blocks[g, :, g, :] for g in range(groups)])
-
-
 MESH = pl.DeviceIdType.MESH
 LEAD = 2
 
@@ -51,9 +44,11 @@
 def token_kernel(
     n, ndp, parts, depth, chunk,
     x_hbm, cot_hbm, w_hbm,
-    out_ref, stats_ref,
+    out_ref, stats_out, sums_out,
+    stats_ref, packed_stats, stats_in, packed_sums, sums_in, products, products_in,
     held, cot, weights, padded, totals, patch_sums, bank,
     send_right, recv_right, send_left, recv_left, w_send, w_recv, local_sem,
+    stats_send, stats_recv, sums_send, sums_recv, products_send, products_recv,
 ):
     me = lax.axis_index("group")
     mine = lax.axis_index("dp")
@@ -199,6 +194,35 @@
             for to_right in (True, False):
                 x_copy(hop, piece, to_right).wait_send()
 
+    def exchange(source, landing, send, recv):
+        return [
+            pltpu.make_async_remote_copy(
+                src_ref=source(lax.rem(mine + step, ndp)),
+                dst_ref=landing.at[mine],
+                send_sem=send.at[step],
+                recv_sem=recv.at[step],
+                device_id={"dp": lax.rem(mine + step, ndp)},
+                device_id_type=MESH,
+            )
+            for step in range(1, ndp)
+        ]
+
+    lane_group = lax.rem(lax.broadcasted_iota(jnp.int32, (GW, 2 * width), 1), width) // GW
+    diagonal = jnp.zeros((GW, 2 * width), jnp.float32)
+    for g in range(width // GW):
+        diagonal = jnp.where(lane_group == g, stats_ref[g * GW : (g + 1) * GW, :], diagonal)
+    packed_stats[:GW, :] = diagonal
+    packed_stats[GW:, :] = stats_ref[width:, :]
+    packed_sums[...] = jnp.zeros_like(packed_sums)
+    for slot in range(n):
+        packed_sums[pl.ds(lax.rem(me - slot + n, n), 1), :] = patch_sums[slot, :1, :]
+    stats_copies = exchange(lambda other: packed_stats, stats_in, stats_send, stats_recv)
+    sums_copies = exchange(lambda other: packed_sums, sums_in, sums_send, sums_recv)
+    for copy in stats_copies + sums_copies:
+        copy.start()
+    stats_in[mine] = packed_stats[...]
+    sums_in[mine] = packed_sums[...]
+
     for slot in range(n):
         origin = lax.rem(me - slot + n, n)
         base = pl.multiple_of(origin * depth, 8)
@@ -207,14 +231,23 @@
             start, size, offset = window_of(part, depth)
             block = totals[slot, part, :, :size].T[offset : offset + depth]
             gathered = block if gathered is None else gathered + block
-        out_ref[pl.ds(base, depth), : 2 * width] = gathered
-        added = None
-        for part in range(parts):
-            start, size, offset = window_of(part, depth)
-            line = jnp.broadcast_to(patch_sums[slot, :1, start : start + size], (128, size)).T
-            line = line[offset : offset + depth]
-            added = line if added is None else added + line
-        out_ref[pl.ds(base, depth), 2 * width :] = added
+        products[pl.ds(base, depth), :] = gathered
+    product_copies = exchange(
+        lambda other: products.at[pl.ds(pl.multiple_of(other * slab, 8), slab)],
+        products_in,
+        products_send,
+        products_recv,
+    )
+    for copy in product_copies:
+        copy.start()
+    products_in[mine] = products[pl.ds(pl.multiple_of(mine * slab, 8), slab), :]
+    for copy in stats_copies + sums_copies:
+        copy.wait()
+    stats_out[...] = sum(stats_in[k] for k in range(ndp))
+    sums_out[...] = sum(sums_in[k] for k in range(ndp))
+    for copy in product_copies:
+        copy.wait()
+    out_ref[...] = sum(products_in[k] for k in range(ndp))
 
 
 def token_products(patches, embed_weight, cotangent):
@@ -235,16 +268,28 @@
     window = max(window_of(q, depth)[1] for q in range(parts))
     anywhere = pl.BlockSpec(memory_space=pl.ANY)
     in_vmem = pl.BlockSpec(memory_space=pltpu.VMEM)
+    slab = embed_weight.shape[0]
+    stats_shape = (GW + 8, 2 * width)
+    sums_shape = (-(-n // 8) * 8, lanes)
+    peers = pltpu.SemaphoreType.DMA((ndp,))
     ring = pltpu.SemaphoreType.DMA((hops, chunks))
     return pl.pallas_call(
         functools.partial(token_kernel, n, ndp, parts, depth, chunk),
         out_shape=(
-            jax.ShapeDtypeStruct((n * depth, 2 * width + 128), jnp.float32),
-            jax.ShapeDtypeStruct((width + 8, 2 * width), jnp.float32),
+            jax.ShapeDtypeStruct((slab, 2 * width), jnp.float32),
+            jax.ShapeDtypeStruct(stats_shape, jnp.float32),
+            jax.ShapeDtypeStruct(sums_shape, jnp.float32),
         ),
         in_specs=[anywhere] * 3,
-        out_specs=(in_vmem, in_vmem),
+        out_specs=(in_vmem,) * 3,
         scratch_shapes=[
+            pltpu.VMEM((width + 8, 2 * width), jnp.float32),
+            pltpu.VMEM(stats_shape, jnp.float32),
+            pltpu.VMEM((ndp,) + stats_shape, jnp.float32),
+            pltpu.VMEM(sums_shape, jnp.float32),
+            pltpu.VMEM((ndp,) + sums_shape, jnp.float32),
+            pltpu.VMEM((n * depth, 2 * width), jnp.float32),
+            pltpu.VMEM((ndp, slab, 2 * width), jnp.float32),
             pltpu.VMEM((n, rows, lanes), jnp.bfloat16),
             pltpu.VMEM((tok_rows, width), jnp.bfloat16),
             pltpu.VMEM((ndp,) + embed_weight.shape, jnp.bfloat16),
@@ -253,9 +298,9 @@
             pltpu.VMEM((n, 8, lanes), jnp.float32),
             pltpu.VMEM((chunk, 2 * width), jnp.bfloat16),
             ring, ring, ring, ring,
-            pltpu.SemaphoreType.DMA((ndp,)),
-            pltpu.SemaphoreType.DMA((ndp,)),
+            peers, peers,
             pltpu.SemaphoreType.DMA((3,)),
+            peers, peers, peers, peers, peers, peers,
         ],
         compiler_params=pltpu.CompilerParams(
             collective_id=0, has_side_effects=True, vmem_limit_bytes=60 << 20
@@ -272,18 +317,23 @@
     gain_here = lax.dynamic_slice_in_dim(
         channel_gain, lax.axis_index("group") * width_here, width_here
     )
-    patch_products, stats = token_products(patches, embed_weight, cotangent)
-    raw_products = block_diagonals(stats[:width_here, :width_here])
-    cross = jnp.swapaxes(block_diagonals(stats[:width_here, width_here:]), 1, 2)
-    sums = stats[width_here]
-    raw_products, cross, sums = lax.psum((raw_products, cross, sums), "dp")
-    patch_products = lax.psum_scatter(patch_products, "dp", scatter_dimension=0, tiled=True)
+    patch_products, stats, packed_sums = token_products(patches, embed_weight, cotangent)
+    n, depth, slab = lax.axis_size("group"), patches.shape[1], embed_weight.shape[0]
+    raw_products = stats[:GW, :width_here].reshape(GW, -1, GW).transpose(1, 0, 2)
+    cross = stats[:GW, width_here:].reshape(GW, -1, GW).transpose(1, 2, 0)
+    sums = stats[GW]
+    patch_sums = jnp.sum(packed_sums[:n].reshape(n, -1, depth), axis=1).reshape(-1)
+    patch_sums = lax.dynamic_slice_in_dim(patch_sums, lax.axis_index("dp") * slab, slab)[:, None]
     return finish(
-        raw_products, cross, sums, patch_products, gain_here, loss_scale, total_tokens, identity
-    )
-
-
-def finish(raw_products, cross, sums, patch_products, gain_here, loss_scale, total_tokens, identity):
+        raw_products, cross, sums, patch_products, patch_sums,
+        gain_here, loss_scale, total_tokens, identity,
+    )
+
+
+def finish(
+    raw_products, cross, sums, patch_products, patch_sums,
+    gain_here, loss_scale, total_tokens, identity,
+):
     width_here = gain_here.shape[0]
     mean_groups = (sums[:width_here] / total_tokens).reshape(-1, GW)
     cot_sums = sums[width_here:].reshape(-1, GW)
@@ -300,7 +350,6 @@
     scale = loss_scale * gain_here
     (grad_cov,) = pullback(cross * gain_here.reshape(-1, GW)[:, :, None])
     symmetric = (grad_cov + jnp.swapaxes(grad_cov, 1, 2)) / total_tokens
-    patch_sums = patch_products[:, 2 * width_here : 2 * width_here + 1]
     rows = patch_products.shape[0]
     feat_part = patch_products[:, :width_here] - patch_sums * mean_groups.reshape(-1)
     cot_part = scale * (

time: 304 us -> 237 us (0.78)
  waiting for transfers between devices: 65.7 us -> 0 us
  Pallas kernels: 179 us -> 207 us
  between operations: 14.5 us -> 1.09 us
  blocking collectives: 12.1 us -> 0 us
  local copies, waits for them, and re-layouts: 11.1 us -> 7.97 us
    psum x1 -> x0, waiting for transfers between devices: 38.4 us -> none  [body(): raw_products, cross, sums = lax.psum((raw_products, cross, sums), 'dp')]
    pallas_call x1, Pallas kernels: 179 us -> 207 us  [token_products(): pl.pallas_call(functools.partial(token_kernel, n, ndp, parts, depth, chun...]
    reduce_scatter x1 -> x0, waiting for transfers between devices: 26.6 us -> none  [body(): lax.psum_scatter(patch_products, 'dp', scatter_dimension=0, tiled=True)]
    psum x1 -> x0, blocking collectives: 12.1 us -> none  [body(): raw_products, cross, sums = lax.psum((raw_products, cross, sums), 'dp')]
  transfers between devices with their start and end apart: 2 -> 0, of which waited for: 2 -> 0; matrix products, arithmetic and copies ran while one was open for 6% -> 0% of each run, Pallas kernels for 0% -> 0%
where the time goes in v3:
time: 237 us
  Pallas kernels  207 us (87%)
  matrix products  15.1 us (6%)
  local copies, waits for them, and re-layouts  7.97 us (3%)
  other arithmetic  5.19 us (2%)
    pallas_call x1, Pallas kernels, token_products(): pl.pallas_call(functools.partial(token_kernel, n, ndp, parts, depth, chun...  207 us
    dot_general x40, matrix products, matmul_batch(): return jnp.einsum('gij,gjk->gik', left, right, precision=highest)  14.5 us

profile of v3, /device:TPU:0, one launch (start us, length us, event | category | flops | bytes accessed | tf_op | source)
XLA Modules:
  0.0 236.6 jit_solution(4508244210350875670)
XLA Ops:
  0.6 2.9 %fusion.50 = (bf16[3328,192]{0,1:T(8,128)(2,1)S(1)}, bf16[3328,192]{0,1:T(8,128)(2,1)}) fusion(bf16[6656,192]{0,1:T(8,128)(2,1)} %param.4), kind=kLoop, calls=%fused_computation.99 | loop fusion | bytes 5111808 | tf_op jit(solution)/shard_map/slice | solution.py:260
  3.5 0.7 copy.191
  4.3 1.7 copy.192
  6.0 2.4 %pad_maximum_fusion.x_hbm = bf16[3328,384]{1,0:T(8,128)(2,1)} fusion(bf16[3328,192]{1,0:T(8,128)(2,1)S(1)} %copy.192, bf16[3328,192]{1,0:T(8,128)(2,1)S(1)} %copy.191), kind=kLoop, calls=%fused_computation | loop fusion | flops 5111808 | bytes 5111808 | tf_op jit(solution)/shard_map/concatenate | solution.py:259
  8.4 207.2 %shard_map.59 = (f32[96,512]{1,0:T(8,128)}, f32[72,512]{1,0:T(8,128)}, f32[8,384]{1,0:T(8,128)}) custom-call(bf16[3328,384]{1,0:T(8,128)(2,1)} %pad_maximum_fusion.x_hbm, bf16[6656,256]{1,0:T(8,128)(2,1)} %cot_hbm.1, bf16[96,256]{1,0:T(8,128)(2,1)} %w_hbm.1), custom_call_target="tpu_custom_call" | custom-call | tf_op jit(solution)/shard_map/pallas_call | solution.py:276
  215.6 0.7 slice_reduce_fusion
  216.4 0.9 fusion.51
  217.9 0.8 dynamic-slice_multiply_fusion
  218.9 0.5 fusion.13
  220.1 0.4 fusion.6
  220.5 0.4 fusion.52
  221.2 0.4 fusion.5
  221.6 0.4 fusion.54
  222.4 0.4 fusion.4
  222.8 0.4 fusion.56
  223.5 0.4 fusion.3
  224.2 0.4 fusion.58
  224.6 0.4 convolution_add_fusion.16
  225.0 0.4 convolution_add_fusion.15
  225.4 0.4 convolution_add_fusion.14
  225.8 0.4 fusion.15
  226.9 0.4 convolution_add_fusion.11
  227.3 0.4 convolution_add_fusion.10
  227.6 0.4 fusion.16
  228.7 0.4 convolution_add_fusion.7
  229.1 0.4 convolution_add_fusion.6
  229.5 0.4 fusion.17
  230.6 0.4 convolution_add_fusion.3
  231.0 0.4 fusion.1
  233.3 0.5 multiply_reduce_fusion
  235.2 0.7 copy.135
  235.9 0.6 reshape.82
  (49 shorter events, 7.8 us)
Async XLA Ops:
  231.4 2.6 %copy-start.1 = (f32[8,384]{1,0:T(8,128)S(1)}, f32[8,384]{1,0:T(8,128)}, u32[]{:S(2)}) copy-start(f32[8,384]{1,0:T(8,128)} %get-tuple-element.7) | copy-start | bytes 36868
  231.4 2.8 %copy-start = (f32[96,512]{1,0:T(8,128)S(1)}, f32[96,512]{1,0:T(8,128)}, u32[]{:S(2)}) copy-start(f32[96,512]{1,0:T(8,128)} %get-tuple-element.6) | copy-start | bytes 589828

commit v4 on v3

--- a/solution.py
+++ b/solution.py
@@ -250,6 +250,422 @@
     out_ref[...] = sum(products_in[k] for k in range(ndp))
 
 
+def handed(piece, chunks):
+    return (lax.rem(piece, 2) == 1) & (piece < 2 * (chunks * 5 // 13))
+
+
+def line_kernel(
+    n, ndp, parts, depth, chunk,
+    x_hbm, cot_hbm, w_hbm,
+    out_ref, stats_out, sums_out,
+    stats, packed_stats, stats_in, packed_sums, sums_in, products, products_in,
+    held, cot, weights, padded, totals, patch_sums, bank,
+    mate_part, mate_stats, whole_sums, mate_products,
+    own_send, own_recv, mid_send, mid_recv, pass_send, pass_recv,
+    out1_send, out1_recv, out2_send, out2_recv, cot_send, cot_recv,
+    w_send, w_recv, local_sem,
+    stats_send, stats_recv, sums_send, sums_recv, products_send, products_recv,
+    mate_send, mate_recv, last_send, last_recv,
+):
+    me = lax.axis_index("group")
+    mine = lax.axis_index("dp")
+    inner = (me == 1) | (me == 2)
+    outer = (me == 0) | (me == 3)
+    mate = me + 1 - 2 * lax.rem(me, 2)
+    across = 3 - me
+    beyond = 3 - mate
+    rows = x_hbm.shape[0]
+    chunks = rows // chunk
+    width = w_hbm.shape[1]
+    slab = w_hbm.shape[0]
+
+    own_x = pltpu.make_async_copy(x_hbm, held.at[me], local_sem.at[0])
+    own_cot = pltpu.make_async_copy(cot_hbm, cot.at[0], local_sem.at[1])
+    own_w = pltpu.make_async_copy(w_hbm, weights.at[0, mine], local_sem.at[2])
+    own_x.start()
+    own_cot.start()
+    own_w.start()
+
+    barrier = pltpu.get_barrier_semaphore()
+    for step in range(1, ndp):
+        pl.semaphore_signal(
+            barrier, inc=1, device_id={"dp": lax.rem(mine + step, ndp)}, device_id_type=MESH
+        )
+    pl.semaphore_signal(barrier, inc=1, device_id={"group": mate}, device_id_type=MESH)
+
+    @pl.when(inner)
+    def _():
+        pl.semaphore_signal(barrier, inc=1, device_id={"group": across}, device_id_type=MESH)
+        pl.semaphore_wait(barrier, ndp + 1)
+
+    @pl.when(outer)
+    def _():
+        pl.semaphore_wait(barrier, ndp)
+
+    def remote(source, target, send, recv, to):
+        return pltpu.make_async_remote_copy(
+            src_ref=source, dst_ref=target, send_sem=send, recv_sem=recv,
+            device_id=to, device_id_type=MESH,
+        )
+
+    def w_copy(step):
+        return remote(
+            w_hbm, weights.at[0, mine], w_send.at[step], w_recv.at[step],
+            {"dp": lax.rem(mine + step, ndp)},
+        )
+
+    def span_of(piece):
+        return pl.ds(pl.multiple_of(piece * chunk, chunk), chunk)
+
+    to_mate, to_across = {"group": mate}, {"group": across}
+
+    def block(origin, piece, send, recv, to, own=False):
+        span = span_of(piece)
+        return remote(
+            x_hbm.at[span] if own else held.at[origin, span],
+            held.at[origin, span], send.at[piece], recv.at[piece], to,
+        )
+
+    def own_copy(piece):
+        return block(me, piece, own_send, own_recv, to_mate, True)
+
+    def mid_copy(piece):
+        return block(me, piece, mid_send, mid_recv, to_across, True)
+
+    def pass_copy(piece):
+        return block(mate, piece, pass_send, pass_recv, to_across)
+
+    def out1_copy(piece):
+        return block(across, piece, out1_send, out1_recv, to_mate)
+
+    def out2_copy(piece):
+        return block(beyond, piece, out2_send, out2_recv, to_mate)
+
+    def cot_copy(piece):
+        span = span_of(piece)
+        return remote(
+            cot_hbm.at[:, span], cot.at[1, :, span], cot_send.at[piece], cot_recv.at[piece],
+            to_mate,
+        )
+
+    mate_w = remote(weights.at[0], weights.at[1], mate_send.at[0], mate_recv.at[0], to_mate)
+    mate_p = remote(mate_part, mate_products, last_send.at[0], last_recv.at[0], to_mate)
+    mate_s = remote(packed_stats.at[1], mate_stats, mate_send.at[1], mate_recv.at[1], to_mate)
+    mate_x = remote(whole_sums, sums_out, last_send.at[1], last_recv.at[1], to_mate)
+
+    for step in range(1, ndp):
+        w_copy(step).start()
+
+    @pl.when(inner)
+    def _():
+        for piece in range(min(LEAD, chunks)):
+            mid_copy(piece).start()
+
+    @pl.when(outer)
+    def _():
+        for piece in range(min(LEAD, chunks)):
+            own_copy(piece).start()
+
+    totals[...] = jnp.zeros_like(totals)
+    patch_sums[...] = jnp.zeros_like(patch_sums)
+    stats[...] = jnp.zeros_like(stats)
+    padded[...] = jnp.zeros_like(padded)
+    own_w.wait()
+    for step in range(1, ndp):
+        w_copy(step).wait()
+    per = depth // slab
+
+    def pad_weights(which):
+        for j in range(n):
+            for part in range(parts):
+                offset = window_of(part, depth)[2]
+                for k in range(per):
+                    padded[which, j, part, offset + k * slab : offset + (k + 1) * slab, :] = (
+                        weights[which, j * per + k]
+                    )
+
+    @pl.when(outer)
+    def _():
+        mate_w.start()
+
+        @pl.loop(0, chunks)
+        def _(piece):
+            @pl.when(piece >= LEAD)
+            def _():
+                own_copy(piece).start()
+
+            @pl.when(handed(piece, chunks))
+            def _():
+                cot_copy(piece).start()
+
+    pad_weights(0)
+    own_x.wait()
+    own_cot.wait()
+    ones = jnp.ones((16, chunk), jnp.bfloat16)
+
+    def compute(piece, which):
+        span = span_of(piece)
+        for part in range(parts):
+            start, size, _ = window_of(part, depth)
+            embedded = jnp.zeros((chunk, width), jnp.float32)
+            for slot in range(n):
+                embedded += jnp.dot(
+                    held[slot, span, start : start + size],
+                    padded[which, slot, part, :size, :],
+                    preferred_element_type=jnp.float32,
+                )
+            bank[:, :width] = embedded.astype(jnp.bfloat16)
+            bank[:, width:] = cot[which, part, span, :]
+            both = bank[...]
+            flipped = both.T
+            stats[which, :width, :] += jnp.dot(
+                flipped[:width], both, preferred_element_type=jnp.float32
+            )
+            stats[which, width:, :] += jnp.dot(ones, both, preferred_element_type=jnp.float32)[:8]
+            for slot in range(n):
+                totals[which, slot, part, :, :size] += jnp.dot(
+                    flipped,
+                    held[slot, span, start : start + size],
+                    preferred_element_type=jnp.float32,
+                )
+
+    def add_sums(piece):
+        for slot in range(n):
+            patch_sums[slot] += jnp.dot(
+                ones, held[slot, span_of(piece), :], preferred_element_type=jnp.float32
+            )[:8]
+
+    def exchange(source, landing, send, recv):
+        return [
+            remote(
+                source(lax.rem(mine + step, ndp)), landing.at[mine],
+                send.at[step], recv.at[step], {"dp": lax.rem(mine + step, ndp)},
+            )
+            for step in range(1, ndp)
+        ]
+
+    def product_copies(which):
+        return exchange(
+            lambda other: products.at[which, pl.ds(pl.multiple_of(other * slab, 8), slab)],
+            products_in.at[which], products_send.at[which], products_recv.at[which],
+        )
+
+    lane_group = lax.rem(lax.broadcasted_iota(jnp.int32, (GW, 2 * width), 1), width) // GW
+
+    def pack_stats(which):
+        diagonal = jnp.zeros((GW, 2 * width), jnp.float32)
+        for g in range(width // GW):
+            diagonal = jnp.where(
+                lane_group == g, stats[which, g * GW : (g + 1) * GW, :], diagonal
+            )
+        packed_stats[which, :GW, :] = diagonal
+        packed_stats[which, GW:, :] = stats[which, width:, :]
+
+    def send_products(which):
+        for slot in range(n):
+            gathered = None
+            for part in range(parts):
+                start, size, offset = window_of(part, depth)
+                rows_here = totals[which, slot, part, :, :size].T[offset : offset + depth]
+                gathered = rows_here if gathered is None else gathered + rows_here
+            products[which, slot * depth : (slot + 1) * depth, :] = gathered
+        for copy in product_copies(which):
+            copy.start()
+        products_in[which, mine] = products[
+            which, pl.ds(pl.multiple_of(mine * slab, 8), slab), :
+        ]
+
+    given = 2 * (chunks * 5 // 13)
+
+    @pl.when(inner)
+    def _():
+        @pl.loop(0, chunks + LEAD)
+        def _(step):
+            @pl.when(step + LEAD < chunks)
+            def _():
+                mid_copy(step + LEAD).start()
+
+            @pl.when(step < chunks)
+            def _():
+                own_copy(step).wait_recv()
+                pass_copy(step).start()
+                mid_copy(step).wait_recv()
+
+                @pl.when(jnp.logical_not(handed(step, chunks)))
+                def _():
+                    own_copy(step).start()
+                    out1_copy(step).start()
+
+            @pl.when(step == LEAD)
+            def _():
+                mate_w.wait_recv()
+                pad_weights(1)
+
+            piece = step - LEAD
+
+            @pl.when(piece >= 0)
+            def _():
+                pass_copy(piece).wait_recv()
+
+                @pl.when(jnp.logical_not(handed(piece, chunks)))
+                def _():
+                    out2_copy(piece).start()
+
+                compute(piece, 0)
+                add_sums(piece)
+
+                @pl.when(handed(piece, chunks))
+                def _():
+                    cot_copy(piece).wait_recv()
+                    compute(piece, 1)
+
+            @pl.when(piece == given)
+            def _():
+                pack_stats(1)
+                mate_s.start()
+                send_products(1)
+
+    @pl.when(outer)
+    def _():
+        @pl.loop(0, chunks)
+        def _(piece):
+            @pl.when(jnp.logical_not(handed(piece, chunks)))
+            def _():
+                own_copy(piece).wait_recv()
+                out1_copy(piece).wait_recv()
+                out2_copy(piece).wait_recv()
+                compute(piece, 0)
+
+        mate_s.wait_recv()
+
+    pack_stats(0)
+
+    @pl.when(outer)
+    def _():
+        packed_stats[0] = packed_stats[0] + mate_stats[...]
+
+    packed_sums[...] = jnp.zeros_like(packed_sums)
+    for slot in range(n):
+        packed_sums[slot : slot + 1, :] = patch_sums[slot, :1, :]
+    stats_copies = exchange(lambda other: packed_stats.at[0], stats_in, stats_send, stats_recv)
+    sums_copies = exchange(lambda other: packed_sums, sums_in, sums_send, sums_recv)
+    for copy in sums_copies + stats_copies:
+        copy.start()
+    stats_in[mine] = packed_stats[0]
+    sums_in[mine] = packed_sums[...]
+    send_products(0)
+
+    @pl.when(inner)
+    def _():
+        for copy in product_copies(1):
+            copy.wait()
+        mate_part[...] = sum(products_in[1, k] for k in range(ndp))
+        mate_p.start()
+
+    for copy in sums_copies:
+        copy.wait()
+    whole_sums[...] = sum(sums_in[k] for k in range(ndp))
+
+    @pl.when(inner)
+    def _():
+        mate_x.start()
+        sums_out[...] = whole_sums[...]
+
+    for copy in stats_copies:
+        copy.wait()
+    stats_out[...] = sum(stats_in[k] for k in range(ndp))
+
+    @pl.loop(0, chunks)
+    def _(piece):
+        @pl.when(inner)
+        def _():
+            mid_copy(piece).wait_send()
+            pass_copy(piece).wait_send()
+
+            @pl.when(jnp.logical_not(handed(piece, chunks)))
+            def _():
+                own_copy(piece).wait_send()
+                out1_copy(piece).wait_send()
+                out2_copy(piece).wait_send()
+
+        @pl.when(outer)
+        def _():
+            own_copy(piece).wait_send()
+
+            @pl.when(handed(piece, chunks))
+            def _():
+                cot_copy(piece).wait_send()
+
+    for copy in product_copies(0):
+        copy.wait()
+    out_ref[...] = sum(products_in[0, k] for k in range(ndp))
+
+    @pl.when(inner)
+    def _():
+        mate_s.wait_send()
+        mate_p.wait_send()
+        mate_x.wait_send()
+
+    @pl.when(outer)
+    def _():
+        mate_w.wait_send()
+        mate_x.wait_recv()
+        mate_p.wait_recv()
+        out_ref[...] = out_ref[...] + mate_products[...]
+
+
+def line_products(packed, cotangent, embed_weight, parts, depth, chunk, stats_shape, sums_shape):
+    n, ndp = lax.axis_size("group"), lax.axis_size("dp")
+    rows, lanes = packed.shape
+    slab, width = embed_weight.shape
+    chunks = rows // chunk
+    window = max(window_of(q, depth)[1] for q in range(parts))
+    anywhere = pl.BlockSpec(memory_space=pl.ANY)
+    in_vmem = pl.BlockSpec(memory_space=pltpu.VMEM)
+    pieces = pltpu.SemaphoreType.DMA((chunks,))
+    peers = pltpu.SemaphoreType.DMA((ndp,))
+    pair = pltpu.SemaphoreType.DMA((2,))
+    both_peers = pltpu.SemaphoreType.DMA((2, ndp))
+    return pl.pallas_call(
+        functools.partial(line_kernel, n, ndp, parts, depth, chunk),
+        out_shape=(
+            jax.ShapeDtypeStruct((slab, 2 * width), jnp.float32),
+            jax.ShapeDtypeStruct(stats_shape, jnp.float32),
+            jax.ShapeDtypeStruct(sums_shape, jnp.float32),
+        ),
+        in_specs=[anywhere] * 3,
+        out_specs=(in_vmem,) * 3,
+        scratch_shapes=[
+            pltpu.VMEM((2, width + 8, 2 * width), jnp.float32),
+            pltpu.VMEM((2,) + stats_shape, jnp.float32),
+            pltpu.VMEM((ndp,) + stats_shape, jnp.float32),
+            pltpu.VMEM(sums_shape, jnp.float32),
+            pltpu.VMEM((ndp,) + sums_shape, jnp.float32),
+            pltpu.VMEM((2, n * depth, 2 * width), jnp.float32),
+            pltpu.VMEM((2, ndp, slab, 2 * width), jnp.float32),
+            pltpu.VMEM((n, rows, lanes), jnp.bfloat16),
+            pltpu.VMEM((2, parts, rows, width), jnp.bfloat16),
+            pltpu.VMEM((2, ndp, slab, width), jnp.bfloat16),
+            pltpu.VMEM((2, n, parts, window, width), jnp.bfloat16),
+            pltpu.VMEM((2, n, parts, 2 * width, window), jnp.float32),
+            pltpu.VMEM((n, 8, lanes), jnp.float32),
+            pltpu.VMEM((chunk, 2 * width), jnp.bfloat16),
+            pltpu.VMEM((slab, 2 * width), jnp.float32),
+            pltpu.VMEM(stats_shape, jnp.float32),
+            pltpu.VMEM(sums_shape, jnp.float32),
+            pltpu.VMEM((slab, 2 * width), jnp.float32),
+            *[pieces] * 12,
+            peers, peers,
+            pltpu.SemaphoreType.DMA((3,)),
+            peers, peers, peers, peers, both_peers, both_peers,
+            pair, pair, pair, pair,
+        ],
+        compiler_params=pltpu.CompilerParams(
+            collective_id=1, has_side_effects=True, vmem_limit_bytes=60 << 20
+        ),
+    )(packed, cotangent.reshape(parts, rows, width), embed_weight)
+
+
 def token_products(patches, embed_weight, cotangent):
     n, ndp = lax.axis_size("group"), lax.axis_size("dp")
     tok_rows, depth = patches.shape
@@ -272,6 +688,10 @@
     stats_shape = (GW + 8, 2 * width)
     sums_shape = (-(-n // 8) * 8, lanes)
     peers = pltpu.SemaphoreType.DMA((ndp,))
+    if n == 4 and 3 <= chunks:
+        return line_products(
+            packed, cotangent, embed_weight, parts, depth, chunk, stats_shape, sums_shape
+        )
     ring = pltpu.SemaphoreType.DMA((hops, chunks))
     return pl.pallas_call(
         functools.partial(token_kernel, n, ndp, parts, depth, chunk),

time: 237 us -> 201 us (0.85)
  Pallas kernels: 207 us -> 171 us
    pallas_call x1, Pallas kernels: 207 us -> 171 us  [line_products(): pl.pallas_call(functools.partial(line_kernel, n, ndp, parts, depth, chunk...]
where the time goes in v4:
time: 201 us; the launch traced here: 200 us
  Pallas kernels  171 us (85%)
  matrix products  15.1 us (8%)
  local copies, waits for them, and re-layouts  7.97 us (4%)
  other arithmetic  5.19 us (3%)
    pallas_call x1, Pallas kernels, line_products(): pl.pallas_call(functools.partial(line_kernel, n, ndp, parts, depth, chunk...  171 us
    dot_general x40, matrix products, matmul_batch(): return jnp.einsum('gij,gjk->gik', left, right, precision=highest)  14.5 us

profile of v4, /device:TPU:0, one launch (start us, length us, event | category | flops | bytes accessed | tf_op | source)
XLA Modules:
  0.0 200.0 jit_solution(10886135072203946476)
XLA Ops:
  0.6 2.9 %fusion.50 = (bf16[3328,192]{0,1:T(8,128)(2,1)S(1)}, bf16[3328,192]{0,1:T(8,128)(2,1)}) fusion(bf16[6656,192]{0,1:T(8,128)(2,1)} %param.4), kind=kLoop, calls=%fused_computation.99 | loop fusion | bytes 5111808 | tf_op jit(solution)/shard_map/slice | solution.py:676
  3.5 0.7 copy.191
  4.3 1.7 copy.192
  6.0 2.4 %pad_maximum_fusion.x_hbm = bf16[3328,384]{1,0:T(8,128)(2,1)} fusion(bf16[3328,192]{1,0:T(8,128)(2,1)S(1)} %copy.192, bf16[3328,192]{1,0:T(8,128)(2,1)S(1)} %copy.191), kind=kLoop, calls=%fused_computation | loop fusion | flops 5111808 | bytes 5111808 | tf_op jit(solution)/shard_map/concatenate | solution.py:675
  8.4 170.7 %shard_map.59 = (f32[96,512]{1,0:T(8,128)}, f32[72,512]{1,0:T(8,128)}, f32[8,384]{1,0:T(8,128)}) custom-call(bf16[3328,384]{1,0:T(8,128)(2,1)} %pad_maximum_fusion.x_hbm, bf16[2,3328,256]{2,1,0:T(8,128)(2,1)} %bitcast.96, bf16[96,256]{1,0:T(8,128)(2,1)} %w_hbm.1), custom_call_target="tpu_custom_call" | custom-call | tf_op jit(solution)/shard_map/pallas_call | solution.py:629
  179.1 0.7 slice_reduce_fusion
  179.9 0.9 fusion.51
  181.4 0.8 dynamic-slice_multiply_fusion
  182.4 0.5 fusion.13
  183.5 0.4 fusion.6
  184.0 0.4 fusion.52
  184.7 0.4 fusion.5
  185.1 0.4 fusion.54
  185.8 0.4 fusion.4
  186.2 0.4 fusion.56
  187.0 0.4 fusion.3
  187.7 0.4 fusion.58
  188.1 0.4 convolution_add_fusion.16
  188.5 0.4 convolution_add_fusion.15
  188.8 0.4 convolution_add_fusion.14
  189.2 0.4 fusion.15
  190.3 0.4 convolution_add_fusion.11
  190.7 0.4 convolution_add_fusion.10
  191.1 0.4 fusion.16
  192.2 0.4 convolution_add_fusion.7
  192.6 0.4 convolution_add_fusion.6
  193.0 0.4 fusion.17
  194.1 0.4 convolution_add_fusion.3
  194.5 0.4 fusion.1
  196.8 0.5 multiply_reduce_fusion
  198.7 0.7 copy.135
  199.4 0.6 reshape.86
  (49 shorter events, 7.8 us)
Async XLA Ops:
  194.9 2.6 %copy-start.1 = (f32[8,384]{1,0:T(8,128)S(1)}, f32[8,384]{1,0:T(8,128)}, u32[]{:S(2)}) copy-start(f32[8,384]{1,0:T(8,128)} %get-tuple-element.7) | copy-start | bytes 36868
  194.9 2.8 %copy-start = (f32[96,512]{1,0:T(8,128)S(1)}, f32[96,512]{1,0:T(8,128)}, u32[]{:S(2)}) copy-start(f32[96,512]{1,0:T(8,128)} %get-tuple-element.6) | copy-start | bytes 589828

commit v5 on v4

--- a/solution.py
+++ b/solution.py
@@ -251,7 +251,7 @@
 
 
 def handed(piece, chunks):
-    return (lax.rem(piece, 2) == 1) & (piece < 2 * (chunks * 5 // 13))
+    return (lax.rem(piece, 2) == 1) & (piece < 2 * (chunks * 6 // 13))
 
 
 def line_kernel(
@@ -475,7 +475,7 @@
             which, pl.ds(pl.multiple_of(mine * slab, 8), slab), :
         ]
 
-    given = 2 * (chunks * 5 // 13)
+    given = 2 * (chunks * 6 // 13)
 
     @pl.when(inner)
     def _():

time: 201 us -> 199 us (0.990)
  the two profiles are of different devices: /device:TPU:0 before, /device:TPU:9 now
where the time goes in v5:
time: 199 us
  Pallas kernels  170 us (85%)
  matrix products  15.1 us (8%)
  local copies, waits for them, and re-layouts  7.97 us (4%)
  other arithmetic  5.19 us (3%)
    pallas_call x1, Pallas kernels, line_products(): pl.pallas_call(functools.partial(line_kernel, n, ndp, parts, depth, chunk...  170 us
    dot_general x40, matrix products, matmul_batch(): return jnp.einsum('gij,gjk->gik', left, right, precision=highest)  14.5 us

profile of v5, /device:TPU:9, one launch (start us, length us, event | category | flops | bytes accessed | tf_op | source)
XLA Modules:
  0.0 198.9 jit_solution(219850279635362217)
XLA Ops:
  0.6 2.9 %fusion.50 = (bf16[3328,192]{0,1:T(8,128)(2,1)S(1)}, bf16[3328,192]{0,1:T(8,128)(2,1)}) fusion(bf16[6656,192]{0,1:T(8,128)(2,1)} %param.4), kind=kLoop, calls=%fused_computation.99 | loop fusion | bytes 5111808 | tf_op jit(solution)/shard_map/slice | solution.py:676
  3.5 0.7 copy.191
  4.3 1.7 copy.192
  6.0 2.4 %pad_maximum_fusion.x_hbm = bf16[3328,384]{1,0:T(8,128)(2,1)} fusion(bf16[3328,192]{1,0:T(8,128)(2,1)S(1)} %copy.192, bf16[3328,192]{1,0:T(8,128)(2,1)S(1)} %copy.191), kind=kLoop, calls=%fused_computation | loop fusion | flops 5111808 | bytes 5111808 | tf_op jit(solution)/shard_map/concatenate | solution.py:675
  8.4 169.5 %shard_map.59 = (f32[96,512]{1,0:T(8,128)}, f32[72,512]{1,0:T(8,128)}, f32[8,384]{1,0:T(8,128)}) custom-call(bf16[3328,384]{1,0:T(8,128)(2,1)} %pad_maximum_fusion.x_hbm, bf16[2,3328,256]{2,1,0:T(8,128)(2,1)} %bitcast.96, bf16[96,256]{1,0:T(8,128)(2,1)} %w_hbm.1), custom_call_target="tpu_custom_call" | custom-call | tf_op jit(solution)/shard_map/pallas_call | solution.py:629
  177.9 0.7 slice_reduce_fusion
  178.7 0.9 fusion.51
  180.2 0.8 dynamic-slice_multiply_fusion
  181.2 0.5 fusion.13
  182.4 0.4 fusion.6
  182.8 0.4 fusion.52
  183.5 0.4 fusion.5
  183.9 0.4 fusion.54
  184.7 0.4 fusion.4
  185.1 0.4 fusion.56
  185.8 0.4 fusion.3
  186.5 0.4 fusion.58
  186.9 0.4 convolution_add_fusion.16
  187.3 0.4 convolution_add_fusion.15
  187.7 0.4 convolution_add_fusion.14
  188.1 0.4 fusion.15
  189.2 0.4 convolution_add_fusion.11
  189.6 0.4 convolution_add_fusion.10
  190.0 0.4 fusion.16
  191.0 0.4 convolution_add_fusion.7
  191.4 0.4 convolution_add_fusion.6
  191.8 0.4 fusion.17
  192.9 0.4 convolution_add_fusion.3
  193.3 0.4 fusion.1
  195.6 0.5 multiply_reduce_fusion
  197.5 0.7 copy.135
  198.2 0.6 reshape.86
  (49 shorter events, 7.8 us)
Async XLA Ops:
  193.7 2.6 %copy-start.1 = (f32[8,384]{1,0:T(8,128)S(1)}, f32[8,384]{1,0:T(8,128)}, u32[]{:S(2)}) copy-start(f32[8,384]{1,0:T(8,128)} %get-tuple-element.7) | copy-start | bytes 36868
  193.7 2.8 %copy-start = (f32[96,512]{1,0:T(8,128)S(1)}, f32[96,512]{1,0:T(8,128)}, u32[]{:S(2)}) copy-start(f32[96,512]{1,0:T(8,128)} %get-tuple-element.6) | copy-start | bytes 589828
